TPU v7x, 32 devices: a whole 2x2x4 slice. The times are simulated.
32 devices in a mesh: row: 8 (over z, x), col: 4 (over y, core).
Axes of the slice: x: 2, y: 2, z: 4, core: 2. Of those that a mesh axis runs over, the one named last changes fastest.
Arguments:
- krylov_block: bfloat16 [64, 16384], P(None, ('row', 'col')), may hold values from -54 to 54
- degree: int32 [16384], P(('row', 'col')), may hold values from 16 to 64
- tile_values: bfloat16 [256, 4, 64, 512], P('row', 'col'), may hold values from -6 to 6
- tile_column: int32 [256, 4, 8], P('row', 'col'), may hold values from 0 to 63
- tile_live: int32 [256, 4, 8], P('row', 'col'), may hold values 0 or 1
Outputs:
- orthonormal: float32 [64, 16384], P(None, ('row', 'col'))
- quotient: float32 [64, 64], replicated
All inputs are finite; a program needn't handle non-finite values. No bound on the sum of `tile_live` on one device may be relied on, other than what follows from the above.
Results may differ from a plain program's by a relative error of at most 0.0032.
Values may be sent and summed in bfloat16 or wider, within the bound.
No kernel may reach another device: no remote copies, remote signals or barrier semaphores. Data moves between devices by JAX's collectives and lax.ppermute only.
A program may use at most 128 MiB of HBM per device.

v0:
```python
import math
import jax
import jax.numpy as jnp
from jax import lax
from jax.sharding import PartitionSpec as P


def gram_of(left, right):
    return lax.dot_general(
        left,
        right,
        (((1,), (1,)), ((), ())),
        precision=lax.Precision.HIGHEST,
        preferred_element_type=jnp.float32,
    )


def on_device(krylov_block, degree, tile_values, tile_column, tile_live):
    vectors = krylov_block.shape[0]
    owned_rows = krylov_block.shape[1]
    block_rows = tile_values.shape[0]
    height = tile_values.shape[2]
    slot_width = tile_values.shape[3]
    sources = lax.axis_size("row")
    groups = lax.axis_size("col")
    per_piece = owned_rows // height
    inv_root = lax.rsqrt(degree.astype(jnp.float32))
    basis_wide = krylov_block.astype(jnp.float32)
    scaled = (basis_wide * inv_root[None, :]).astype(jnp.bfloat16)
    gathered = lax.all_gather(scaled, "row", axis=1, tiled=True)
    blocks = gathered.reshape(vectors, sources * per_piece, height)
    pick_index = tile_column[:, 0, :].reshape(-1)
    chosen = jnp.take(blocks, pick_index, axis=1)
    chosen = chosen * tile_live[:, 0, :].reshape(1, -1, 1).astype(jnp.bfloat16)
    chosen = chosen.reshape(vectors, block_rows, slot_width)
    panel = tile_values[:, 0]
    whole_rows = jnp.einsum("klc,luc->klu", chosen, panel, preferred_element_type=jnp.float32)
    whole_rows = whole_rows.reshape(vectors, block_rows * height)
    spread = lax.psum_scatter(whole_rows, "col", scatter_dimension=1, tiled=True)
    applied = basis_wide - inv_root[None, :] * spread
    quotient, energy = lax.psum(
        (gram_of(basis_wide, applied), gram_of(applied, applied)), ("row", "col")
    )
    factor = jnp.linalg.cholesky(energy)
    identity = jnp.eye(vectors, dtype=jnp.float32)
    inverse = lax.linalg.triangular_solve(factor, identity, left_side=True, lower=True)
    total_rows = sources * groups * owned_rows
    orthonormal = jnp.dot(inverse, applied, precision=lax.Precision.HIGHEST) * math.sqrt(total_rows)
    return (orthonormal, quotient / total_rows)


def solution(mesh):
    return jax.shard_map(
        on_device,
        mesh=mesh,
        in_specs=(
            P(None, ("row", "col")),
            P(("row", "col")),
            P("row", "col", None, None),
            P("row", "col", None),
            P("row", "col", None),
        ),
        out_specs=(P(None, ("row", "col")), P()),
        check_vma=False,
    )
```

profile of v0, /device:TPU:0, one launch (start us, length us, event | category | flops | bytes accessed | tf_op | source)
XLA Modules:
  0.0 156.6 jit_solution(8631686106743871151)
XLA Ops:
  7.2 0.9 copy.22
  8.1 0.7 compare_and_fusion
  8.8 0.7 convert_rsqrt_fusion
  9.5 0.9 fusion.8
  10.4 33.0 %all_gather.3 = bf16[64,4096]{1,0:T(8,128)(2,1)S(1)} all-gather(bf16[64,512]{1,0:T(8,128)(2,1)S(1)} %fusion.8), channel_id=1, replica_groups=mesh['row'=8,'col'=4] {'row'}, dimensions={1}, use_global_device_ids=true | all-gather | bytes 589824 | tf_op jit(solution)/shard_map/all_gather | solution.py:30
  43.4 2.1 %reshape.72 = bf16[64,64,64]{2,1,0:T(8,128)(2,1)} reshape(bf16[64,4096]{1,0:T(8,128)(2,1)S(1)} %all_gather.3) | data formatting | bytes 1048576 | tf_op jit(solution)/shard_map/reshape | solution.py:31
  45.5 1.9 %copy.23 = bf16[64,64,64]{2,0,1:T(8,128)(2,1)S(1)} copy(bf16[64,64,64]{2,1,0:T(8,128)(2,1)} %reshape.72) | data formatting | bytes 1048576 | tf_op jit(solution)/shard_map/reshape | solution.py:31
  47.4 0.1 reshape_squeeze.7
  47.5 3.1 %gather_fusion = bf16[256,64,64]{2,1,0:T(8,128)(2,1)} fusion(bf16[64,64,64]{2,0,1:T(8,128)(2,1)S(1)} %copy.23, s32[1024]{0:T(1024)S(1)} %pad_clamp_fusion), kind=kCustom, calls=%fused_computation | custom fusion | bytes 4195328 | tf_op jit(solution)/shard_map/jit(_take)/gather | solution.py:33
  50.6 6.8 %copy.24 = bf16[64,256,64]{2,1,0:T(8,128)(2,1)} copy(bf16[64,256,64]{2,0,1:T(8,128)(2,1)} %bitcast.30) | data formatting | bytes 4194304 | tf_op jit(solution)/shard_map/jit(_take)/gather | solution.py:33
  57.4 6.5 %gather.7 = bf16[64,32,512]{2,1,0:T(8,128)(2,1)} reshape(bf16[64,256,64]{2,1,0:T(8,128)(2,1)} %copy.24) | data formatting | bytes 4194304 | tf_op jit(solution)/shard_map/jit(_take)/gather | solution.py:33
  63.9 0.1 copy.25
  64.0 0.1 mul.35
  64.1 0.1 mul.36
  64.2 0.1 copy.21
  64.3 0.1 broadcast_in_dim.18
  64.4 0.1 broadcast_in_dim.19
  64.5 1.8 %select_multiply_fusion = bf16[64,32,512]{2,1,0:T(8,128)(2,1)S(1)} fusion(bf16[64,32,512]{2,1,0:T(8,128)(2,1)} %gather.7, pred[32,512]{1,0:T(8,128)(4,1)S(1)} %broadcast_in_dim.19, bf16[32,512]{1,0:T(8,128)(2,1)S(1)} %mul.36), kind=kLoop, calls=%fused_computation.4 | loop fusion | flops 2097152 | bytes 4243456 | tf_op jit(solution)/shard_map/mul | solution.py:34
  66.3 1.4 fusion.3
  67.7 0.6 copy.27
  68.4 1.1 reshape.73
  69.5 22.9 %reduce-scatter.2.cloned.1.call-done = f32[64,512]{1,0:T(8,128)} async-done(((f32[64,2048]{1,0:T(8,128)}), f32[64,512]{1,0:T(8,128)}) %reduce-scatter.2.cloned.1.call-update) | async-done | bytes 131088 | tf_op jit(solution)/shard_map/reduce_scatter | solution.py:39
  92.5 1.1 convolution_bitcast_fusion
  93.6 1.3 fusion.9
  94.8 40.0 %all-reduce = (f32[64,64]{0,1:T(8,128)S(1)}, f32[64,64]{0,1:T(8,128)S(1)}) all-reduce(f32[64,64]{0,1:T(8,128)S(1)} %fusion.9, f32[64,64]{0,1:T(8,128)S(1)} %convolution_bitcast_fusion), channel_id=1, replica_groups=mesh['row'=8,'col'=4] {'row','col'}, use_global_device_ids=true, to_apply=%region_1.2 | all-reduce | flops 8192 | bytes 65536 | tf_op jit(solution)/shard_map/psum | solution.py:41
  134.9 5.8 %cholesky.17 = f32[64,64]{1,0:T(8,128)S(1)} custom-call(f32[64,64]{1,0:T(8,128)S(1)} %fusion.16), custom_call_target="Cholesky" | custom-call | tf_op jit(solution)/shard_map/jit(cholesky)/cholesky | solution.py:44
  140.8 0.6 compare_reduce_fusion
  141.4 0.7 fusion.13
  142.1 4.9 %custom-call.6 = f32[1,64,64]{1,2,0:T(8,128)S(1)} custom-call(f32[1,64,64]{2,1,0:T(8,128)S(1)} %fusion.13), custom_call_target="InvertDiagBlocksLowerTriangular" | custom-call | tf_op jit(solution)/shard_map/triangular_solve | solution.py:46
  147.0 0.2 fusion.14
  147.3 0.7 copy.30
  148.0 1.8 %convolution_multiply_fusion = f32[64,512]{1,0:T(8,128)} fusion(f32[64,64]{1,0:T(8,128)S(1)} %fusion.14, bf16[64,512]{1,0:T(8,128)(2,1)S(1)} %copy-done.1, f32[64,512]{1,0:T(8,128)} %reduce-scatter.2.cloned.1.call-done, f32[512]{0:T(512)S(1)} %convert_rsqrt_fusion), kind=kOutput, calls=%fused_computation.6 | convolution fusion | flops 25296896 | bytes 346112 | tf_op jit(solution)/shard_map/dot_general | solution.py:48
  (15 shorter events, 0.2 us)
Async XLA Ops:
  7.2 59.1 %copy-start = (bf16[32,1,64,512]{3,2,1,0:T(8,128)(2,1)S(1)}, bf16[32,1,64,512]{3,2,1,0:T(8,128)(2,1)}, u32[]{:S(2)}) copy-start(bf16[32,1,64,512]{3,2,1,0:T(8,128)(2,1)} %param.7) | copy-start | bytes 6291460
  7.2 85.3 %reduce-scatter.2.cloned.1.call-start = ((), (), s32[]{:S(2)}) async-start(), calls=%async_computation.1 | async-start | bytes 655360 | tf_op jit(solution)/shard_map/reduce_scatter | solution.py:39
  57.4 6.5 %copy-start.2 = (s32[32,1,8]{0,2,1:T(8,128)S(1)}, s32[32,1,8]{0,2,1:T(8,128)}, u32[]{:S(2)}) copy-start(s32[32,1,8]{0,2,1:T(8,128)} %param.9) | copy-start | bytes 3076
  67.7 24.7 %copy-start.1 = (bf16[64,512]{1,0:T(8,128)(2,1)S(1)}, bf16[64,512]{1,0:T(8,128)(2,1)}, u32[]{:S(2)}) copy-start(bf16[64,512]{1,0:T(8,128)(2,1)} %param.5) | copy-start | bytes 196612
Sparse Core Ops, SparseCore 0:
  69.7 22.7 reduce-scatter.1
where the time goes:
time: 157 us
  blocking collectives  73 us (46%)
  local copies, waits for them, and re-layouts  24.5 us (16%)
  waiting for transfers between devices  22.9 us (15%)
  other arithmetic  16.1 us (10%)
  between operations  14.1 us (9%)
  matrix products  5.85 us (4%)
    psum x1, blocking collectives, on_device(): lax.psum((gram_of(basis_wide, applied), gram_of(applied, applied)), ('row...  40 us
    all_gather x1, blocking collectives, on_device(): gathered = lax.all_gather(scaled, 'row', axis=1, tiled=True)  33 us
    reduce_scatter x1, waiting for transfers between devices, on_device(): lax.psum_scatter(whole_rows, 'col', scatter_dimension=1, tiled=True)  22.9 us
    gather x3, local copies, waits for them, and re-layouts, on_device(): chosen = jnp.take(blocks, pick_index, axis=1)  16.3 us
    another operation x3, other arithmetic, on_device(): factor = jnp.linalg.cholesky(energy)  6.52 us
    another operation x2, other arithmetic, on_device(): lax.linalg.triangular_solve(factor, identity, left_side=True, lower=True)  5.55 us
    reshape x2, local copies, waits for them, and re-layouts, on_device(): blocks = gathered.reshape(vectors, sources * per_piece, height)  4.01 us
  transfers between devices with their start and end apart: 1, of which 1 were waited for; matrix products, arithmetic and copies ran while one was open for 0% of the time, Pallas kernels for 0%

commit v1 on v0

--- a/solution.py
+++ b/solution.py
@@ -3,6 +3,27 @@
 import jax.numpy as jnp
 from jax import lax
 from jax.sharding import PartitionSpec as P
+
+
+def joined_along(tiles, dim):
+    shape = list(tiles.shape[1:])
+    shape[dim] *= tiles.shape[0]
+    return jnp.moveaxis(tiles, 0, dim).reshape(shape)
+
+
+def grow_blocks(x, axis):
+    count, mine = (lax.axis_size(axis), lax.axis_index(axis))
+    blocks, apart = (x[None], 1)
+    while apart < count:
+        other = lax.ppermute(blocks, axis, [(i, i ^ apart) for i in range(count)])
+        low = mine & apart == 0
+        blocks = jnp.concatenate([jnp.where(low, blocks, other), jnp.where(low, other, blocks)])
+        apart *= 2
+    return blocks
+
+
+def collect(x, axis, dim):
+    return joined_along(grow_blocks(x, axis), dim)
 
 
 def gram_of(left, right):
@@ -27,7 +48,7 @@
     inv_root = lax.rsqrt(degree.astype(jnp.float32))
     basis_wide = krylov_block.astype(jnp.float32)
     scaled = (basis_wide * inv_root[None, :]).astype(jnp.bfloat16)
-    gathered = lax.all_gather(scaled, "row", axis=1, tiled=True)
+    gathered = collect(scaled, "row", 1)
     blocks = gathered.reshape(vectors, sources * per_piece, height)
     pick_index = tile_column[:, 0, :].reshape(-1)
     chosen = jnp.take(blocks, pick_index, axis=1)

time: 157 us -> 146 us (0.930)
  blocking collectives: 73 us -> 40 us
  waiting for transfers between devices: 22.9 us -> 34.9 us
  starting transfers between devices: 0.04 us -> 8.31 us
  other arithmetic: 16.1 us -> 18 us
    all_gather x1 -> x0, blocking collectives: 33 us -> none  [on_device(): gathered = lax.all_gather(scaled, 'row', axis=1, tiled=True)]
    ppermute x0 -> x3, waiting for transfers between devices: none -> 12 us  [grow_blocks(): other = lax.ppermute(blocks, axis, [(i, i ^ apart) for i in range(count)])]
    ppermute x0 -> x3, starting transfers between devices: none -> 8.27 us  [grow_blocks(): other = lax.ppermute(blocks, axis, [(i, i ^ apart) for i in range(count)])]
    reshape x2 -> x0, local copies, waits for them, and re-layouts: 4.01 us -> none  [on_device(): blocks = gathered.reshape(vectors, sources * per_piece, height)]
    another operation x0 -> x2, local copies, waits for them, and re-layouts: none -> 3.44 us  [on_device(): blocks = gathered.reshape(vectors, sources * per_piece, height)]
  transfers between devices with their start and end apart: 1 -> 4, of which waited for: 1 -> 4; matrix products, arithmetic and copies ran while one was open for 0% -> 2% of each run, Pallas kernels for 0% -> 0%
where the time goes in v1:
time: 146 us; the launch traced here: 145 us
  blocking collectives  40 us (27%)
  waiting for transfers between devices  34.9 us (24%)
  local copies, waits for them, and re-layouts  24.1 us (17%)
  other arithmetic  18 us (12%)
  between operations  14.2 us (10%)
  starting transfers between devices  8.31 us (6%)
  matrix products  5.85 us (4%)
    psum x1, blocking collectives, on_device(): lax.psum((gram_of(basis_wide, applied), gram_of(applied, applied)), ('row...  40 us
    reduce_scatter x1, waiting for transfers between devices, on_device(): lax.psum_scatter(whole_rows, 'col', scatter_dimension=1, tiled=True)  23 us
    gather x3, local copies, waits for them, and re-layouts, on_device(): chosen = jnp.take(blocks, pick_index, axis=1)  16.3 us
    ppermute x3, waiting for transfers between devices, grow_blocks(): other = lax.ppermute(blocks, axis, [(i, i ^ apart) for i in range(count)])  12 us
    ppermute x3, starting transfers between devices, grow_blocks(): other = lax.ppermute(blocks, axis, [(i, i ^ apart) for i in range(count)])  8.27 us
    another operation x3, other arithmetic, on_device(): factor = jnp.linalg.cholesky(energy)  6.52 us
    another operation x2, other arithmetic, on_device(): lax.linalg.triangular_solve(factor, identity, left_side=True, lower=True)  5.55 us
    another operation x2, local copies, waits for them, and re-layouts, on_device(): blocks = gathered.reshape(vectors, sources * per_piece, height)  3.44 us
  transfers between devices with their start and end apart: 4, of which 4 were waited for; matrix products, arithmetic and copies ran while one was open for 2% of the time, Pallas kernels for 0%

profile of v1, /device:TPU:0, one launch (start us, length us, event | category | flops | bytes accessed | tf_op | source)
XLA Modules:
  0.0 145.4 jit_solution(439240201845718929)
XLA Ops:
  7.2 0.8 convert_rsqrt_fusion
  8.1 0.9 fusion.10
  8.9 3.0 %collective-permute-start = (bf16[1,64,512]{2,1,0:T(8,128)(2,1)S(1)}, bf16[1,64,512]{2,1,0:T(8,128)(2,1)S(1)}, u32[]{:S(2)}, u32[]{:S(2)}) collective-permute-start(bf16[1,64,512]{2,1,0:T(8,128)(2,1)S(1)} %fusion.10), channel_id=1, source_target_pairs={{0,4},{4,0},{8,12},{12,8},{16,20},{20,16},{24,28},{28,24},{1,5},{5... | collective-permute-start | bytes 196616 | tf_op jit(solution)/shard_map/ppermute | solution.py:18
  11.9 0.7 convert_bitcast_fusion
  12.6 0.8 copy.14
  13.8 0.4 collective-permute-done
  14.2 0.9 broadcast_select_fusion.5
  15.1 2.2 %collective-permute-start.1 = (bf16[2,64,512]{2,1,0:T(8,128)(2,1)S(1)}, bf16[2,64,512]{2,1,0:T(8,128)(2,1)S(1)}, u32[]{:S(2)}, u32[]{:S(2)}) collective-permute-start(bf16[2,64,512]{2,1,0:T(8,128)(2,1)S(1)} %pad_maximum_fusion.1), channel_id=1, source_target_pairs={{0,8},{4,12},{8,0},{12,4},{16,24},{20,28},{24,16},{28,20},{1,9},{5... | collective-permute-start | bytes 393224 | tf_op jit(solution)/shard_map/ppermute | solution.py:18
  17.2 0.7 compare_and_fusion
  18.2 1.9 %collective-permute-done.1 = bf16[2,64,512]{2,1,0:T(8,128)(2,1)S(1)} collective-permute-done((bf16[2,64,512]{2,1,0:T(8,128)(2,1)S(1)}, bf16[2,64,512]{2,1,0:T(8,128)(2,1)S(1)}, u32[]{:S(2)}, u32[]{:S(2)}) %collective-permute-start.1) | collective-permute-done | bytes 131104 | tf_op jit(solution)/shard_map/ppermute | solution.py:18
  20.2 3.1 %collective-permute-start.2 = (bf16[4,64,512]{2,1,0:T(8,128)(2,1)S(1)}, bf16[4,64,512]{2,1,0:T(8,128)(2,1)S(1)}, u32[]{:S(2)}, u32[]{:S(2)}) collective-permute-start(bf16[4,64,512]{2,1,0:T(8,128)(2,1)S(1)} %pad_maximum_fusion), channel_id=1, source_target_pairs={{0,16},{4,20},{8,24},{12,28},{16,0},{20,4},{24,8},{28,12},{1,17},{... | collective-permute-start | bytes 786440 | tf_op jit(solution)/shard_map/ppermute | solution.py:18
  23.3 9.6 %collective-permute-done.2 = bf16[4,64,512]{2,1,0:T(8,128)(2,1)S(1)} collective-permute-done((bf16[4,64,512]{2,1,0:T(8,128)(2,1)S(1)}, bf16[4,64,512]{2,1,0:T(8,128)(2,1)S(1)}, u32[]{:S(2)}, u32[]{:S(2)}) %collective-permute-start.2) | collective-permute-done | bytes 262176 | tf_op jit(solution)/shard_map/ppermute | solution.py:18
  33.1 0.3 copy.13
  33.4 1.5 %reshape_reshape.3 = bf16[64,64,64]{2,1,0:T(8,128)(2,1)} reshape(bf16[64,8,512]{2,1,0:T(8,128)(2,1)S(1)} %copy.13) | data formatting | bytes 1048576 | tf_op jit(solution)/shard_map/reshape;reshape | solution.py:52
  34.9 1.9 %copy.15 = bf16[64,64,64]{2,0,1:T(8,128)(2,1)S(1)} copy(bf16[64,64,64]{2,1,0:T(8,128)(2,1)} %reshape_reshape.3) | data formatting | bytes 1048576 | tf_op jit(solution)/shard_map/reshape;reshape | solution.py:52
  36.8 3.1 %gather_fusion = bf16[256,64,64]{2,1,0:T(8,128)(2,1)} fusion(bf16[64,64,64]{2,0,1:T(8,128)(2,1)S(1)} %copy.15, s32[1024]{0:T(1024)S(1)} %pad_clamp_fusion), kind=kCustom, calls=%fused_computation | custom fusion | bytes 4195328 | tf_op jit(solution)/shard_map/jit(_take)/gather | solution.py:54
  39.9 6.8 %copy.16 = bf16[64,256,64]{2,1,0:T(8,128)(2,1)} copy(bf16[64,256,64]{2,0,1:T(8,128)(2,1)} %bitcast.36) | data formatting | bytes 4194304 | tf_op jit(solution)/shard_map/jit(_take)/gather | solution.py:54
  46.7 6.5 %gather.7 = bf16[64,32,512]{2,1,0:T(8,128)(2,1)} reshape(bf16[64,256,64]{2,1,0:T(8,128)(2,1)} %copy.16) | data formatting | bytes 4194304 | tf_op jit(solution)/shard_map/jit(_take)/gather | solution.py:54
  53.2 1.8 %select_multiply_fusion = bf16[64,32,512]{2,1,0:T(8,128)(2,1)S(1)} fusion(bf16[64,32,512]{2,1,0:T(8,128)(2,1)} %gather.7, pred[32,512]{1,0:T(8,128)(4,1)S(1)} %broadcast_in_dim.22, bf16[32,512]{1,0:T(8,128)(2,1)S(1)} %mul.36), kind=kLoop, calls=%fused_computation.4 | loop fusion | flops 2097152 | bytes 4243456 | tf_op jit(solution)/shard_map/mul | solution.py:55
  55.0 1.4 fusion.3
  56.4 0.6 copy.19
  57.0 1.1 reshape.69
  58.2 23.0 %reduce-scatter.2.cloned.1.call-done = f32[64,512]{1,0:T(8,128)} async-done(((f32[64,2048]{1,0:T(8,128)}), f32[64,512]{1,0:T(8,128)}) %reduce-scatter.2.cloned.1.call-update) | async-done | bytes 131088 | tf_op jit(solution)/shard_map/reduce_scatter | solution.py:60
  81.2 1.1 convolution_bitcast_fusion
  82.3 1.3 fusion.9
  83.5 40.0 %all-reduce = (f32[64,64]{0,1:T(8,128)S(1)}, f32[64,64]{0,1:T(8,128)S(1)}) all-reduce(f32[64,64]{0,1:T(8,128)S(1)} %fusion.9, f32[64,64]{0,1:T(8,128)S(1)} %convolution_bitcast_fusion), channel_id=1, replica_groups=mesh['row'=8,'col'=4] {'row','col'}, use_global_device_ids=true, to_apply=%region_1.2 | all-reduce | flops 8192 | bytes 65536 | tf_op jit(solution)/shard_map/psum | solution.py:62
  123.6 5.8 %cholesky.17 = f32[64,64]{1,0:T(8,128)S(1)} custom-call(f32[64,64]{1,0:T(8,128)S(1)} %fusion.17), custom_call_target="Cholesky" | custom-call | tf_op jit(solution)/shard_map/jit(cholesky)/cholesky | solution.py:65
  129.5 0.6 compare_reduce_fusion
  130.2 0.7 fusion.14
  130.8 4.9 %custom-call.6 = f32[1,64,64]{1,2,0:T(8,128)S(1)} custom-call(f32[1,64,64]{2,1,0:T(8,128)S(1)} %fusion.14), custom_call_target="InvertDiagBlocksLowerTriangular" | custom-call | tf_op jit(solution)/shard_map/triangular_solve | solution.py:67
  136.0 0.7 copy.22
  136.7 1.8 %convolution_multiply_fusion = f32[64,512]{1,0:T(8,128)} fusion(f32[64,64]{1,0:T(8,128)S(1)} %fusion.15, bf16[64,512]{1,0:T(8,128)(2,1)S(1)} %copy-done.1, f32[64,512]{1,0:T(8,128)} %reduce-scatter.2.cloned.1.call-done, f32[512]{0:T(512)S(1)} %convert_rsqrt_fusion), kind=kOutput, calls=%fused_computation.6 | convolution fusion | flops 25296896 | bytes 346112 | tf_op jit(solution)/shard_map/dot_general | solution.py:69
  (25 shorter events, 1.3 us)
Async XLA Ops:
  7.2 47.8 %copy-start = (bf16[32,1,64,512]{3,2,1,0:T(8,128)(2,1)S(1)}, bf16[32,1,64,512]{3,2,1,0:T(8,128)(2,1)}, u32[]{:S(2)}) copy-start(bf16[32,1,64,512]{3,2,1,0:T(8,128)(2,1)} %param.7) | copy-start | bytes 6291460
  7.2 74.0 %reduce-scatter.2.cloned.1.call-start = ((), (), s32[]{:S(2)}) async-start(), calls=%async_computation.1 | async-start | bytes 655360 | tf_op jit(solution)/shard_map/reduce_scatter | solution.py:60
  8.9 5.2 %collective-permute-start = (bf16[1,64,512]{2,1,0:T(8,128)(2,1)S(1)}, bf16[1,64,512]{2,1,0:T(8,128)(2,1)S(1)}, u32[]{:S(2)}, u32[]{:S(2)}) collective-permute-start(bf16[1,64,512]{2,1,0:T(8,128)(2,1)S(1)} %fusion.10), channel_id=1, source_target_pairs={{0,4},{4,0},{8,12},{12,8},{16,20},{20,16},{24,28},{28,24},{1,5},{5... | collective-permute-start | bytes 196616 | tf_op jit(solution)/shard_map/ppermute | solution.py:18
  15.1 5.1 %collective-permute-start.1 = (bf16[2,64,512]{2,1,0:T(8,128)(2,1)S(1)}, bf16[2,64,512]{2,1,0:T(8,128)(2,1)S(1)}, u32[]{:S(2)}, u32[]{:S(2)}) collective-permute-start(bf16[2,64,512]{2,1,0:T(8,128)(2,1)S(1)} %pad_maximum_fusion.1), channel_id=1, source_target_pairs={{0,8},{4,12},{8,0},{12,4},{16,24},{20,28},{24,16},{28,20},{1,9},{5... | collective-permute-start | bytes 393224 | tf_op jit(solution)/shard_map/ppermute | solution.py:18
  20.2 12.7 %collective-permute-start.2 = (bf16[4,64,512]{2,1,0:T(8,128)(2,1)S(1)}, bf16[4,64,512]{2,1,0:T(8,128)(2,1)S(1)}, u32[]{:S(2)}, u32[]{:S(2)}) collective-permute-start(bf16[4,64,512]{2,1,0:T(8,128)(2,1)S(1)} %pad_maximum_fusion), channel_id=1, source_target_pairs={{0,16},{4,20},{8,24},{12,28},{16,0},{20,4},{24,8},{28,12},{1,17},{... | collective-permute-start | bytes 786440 | tf_op jit(solution)/shard_map/ppermute | solution.py:18
  56.4 24.8 %copy-start.1 = (bf16[64,512]{1,0:T(8,128)(2,1)S(1)}, bf16[64,512]{1,0:T(8,128)(2,1)}, u32[]{:S(2)}) copy-start(bf16[64,512]{1,0:T(8,128)(2,1)} %param.5) | copy-start | bytes 196612
Sparse Core Ops, SparseCore 0:
  58.3 22.8 reduce-scatter.1
